TPU v7x, 32 devices: a whole 2x2x4 slice. The times are simulated.
32 devices in a mesh: seq: 4 (over x, core), fsdp: 8 (over z, y).
Axes of the slice: x: 2, y: 2, z: 4, core: 2. Of those that a mesh axis runs over, the one named last changes fastest.
Arguments:
- layer_input: bfloat16 [8, 1536, 1024], P('fsdp', 'seq'), may hold values from -12 to 12
- query_weight: bfloat16 [1024, 1024], P('fsdp'), may hold values from -0.1875 to 0.1875
- key_weight: bfloat16 [1024, 1024], P('fsdp'), may hold values from -0.1875 to 0.1875
- value_weight: bfloat16 [1024, 1024], P('fsdp'), may hold values from -0.1875 to 0.1875
- output_weight: bfloat16 [1024, 1024], P('fsdp'), may hold values from -0.75 to 0.75
- query_bias: bfloat16 [1024], P('fsdp'), may hold values from -4 to 4
- value_bias: bfloat16 [1024], P('fsdp'), may hold values from -1.5 to 1.5
- output_bias: bfloat16 [1024], P('fsdp'), may hold values from -4 to 4
- attn_gain: bfloat16 [1024], P('fsdp'), may hold values from 0.5 to 1.5
- attn_shift: bfloat16 [1024], P('fsdp'), may hold values from -4 to 4
- in_weight: bfloat16 [1024, 4096], P('fsdp'), may hold values from -0.1875 to 0.1875
- in_bias: bfloat16 [4096], P('fsdp'), may hold values from -4 to 4
- out_weight: bfloat16 [4096, 1024], P('fsdp'), may hold values from -0.09375 to 0.09375
- out_bias: bfloat16 [1024], P('fsdp'), may hold values from -4 to 4
- out_gain: bfloat16 [1024], P('fsdp'), may hold values from 0.5 to 1.5
- out_shift: bfloat16 [1024], P('fsdp'), may hold values from -4 to 4
- out_cotangent: bfloat16 [8, 1536, 1024], P('fsdp', 'seq'), may hold values from -6 to 6
Outputs:
- layer_output: bfloat16 [8, 1536, 1024], P('fsdp', 'seq')
- input_grad: float32 [8, 1536, 1024], P('fsdp', 'seq')
- query_weight_grad: float32 [1024, 1024], P('fsdp')
- key_weight_grad: float32 [1024, 1024], P('fsdp')
- value_weight_grad: float32 [1024, 1024], P('fsdp')
- output_weight_grad: float32 [1024, 1024], P('fsdp')
- query_bias_grad: float32 [1024], P('fsdp')
- value_bias_grad: float32 [1024], P('fsdp')
- output_bias_grad: float32 [1024], P('fsdp')
- attn_gain_grad: float32 [1024], P('fsdp')
- attn_shift_grad: float32 [1024], P('fsdp')
- in_weight_grad: float32 [1024, 4096], P('fsdp')
- in_bias_grad: float32 [4096], P('fsdp')
- out_weight_grad: float32 [4096, 1024], P('fsdp')
- out_bias_grad: float32 [1024], P('fsdp')
- out_gain_grad: float32 [1024], P('fsdp')
- out_shift_grad: float32 [1024], P('fsdp')
- rms_values: float32 [5], replicated
All inputs are finite; a program needn't handle non-finite values.
Results may differ from a plain program's by a relative error of at most 0.015.
Values may be sent and summed in bfloat16 or wider, within the bound.
A program may use at most 192 MiB of HBM per device.

v0:
```python
import jax
import jax.numpy as jnp
from jax import lax
from jax.sharding import PartitionSpec as P

HD = 64


def layer_norm(stream, gain, shift):
    centre = stream - jnp.mean(stream, axis=-1, keepdims=True)
    variance = jnp.mean(centre * centre, axis=-1, keepdims=True)
    return centre * lax.rsqrt(variance + 1e-05) * gain + shift


def gelu_exact(inputs):
    return jax.nn.gelu(inputs, approximate=False)


def column_sums(matrix):
    return jnp.sum(matrix.astype(jnp.float32), axis=0)


def local(
    layer_input,
    query_weight,
    key_weight,
    value_weight,
    output_weight,
    query_bias,
    value_bias,
    output_bias,
    attn_gain,
    attn_shift,
    in_weight,
    in_bias,
    out_weight,
    out_bias,
    out_gain,
    out_shift,
    out_cotangent,
):
    half = jnp.bfloat16
    single = jnp.float32
    fsdp_count = lax.axis_size("fsdp")
    seq_count = lax.axis_size("seq")
    (
        full_query,
        full_key,
        full_value,
        full_output,
        bias_query,
        bias_value,
        bias_output,
        gain_one,
        shift_one,
    ) = (
        lax.all_gather(query_weight, "fsdp", axis=0, tiled=True),
        lax.all_gather(key_weight, "fsdp", axis=0, tiled=True),
        lax.all_gather(value_weight, "fsdp", axis=0, tiled=True),
        lax.all_gather(output_weight, "fsdp", axis=0, tiled=True),
        lax.all_gather(query_bias, "fsdp", axis=0, tiled=True),
        lax.all_gather(value_bias, "fsdp", axis=0, tiled=True),
        lax.all_gather(output_bias, "fsdp", axis=0, tiled=True),
        lax.all_gather(attn_gain, "fsdp", axis=0, tiled=True),
        lax.all_gather(attn_shift, "fsdp", axis=0, tiled=True),
    )
    full_in, full_out, bias_in, bias_out, gain_two, shift_two = (
        lax.all_gather(in_weight, "fsdp", axis=0, tiled=True),
        lax.all_gather(out_weight, "fsdp", axis=0, tiled=True),
        lax.all_gather(in_bias, "fsdp", axis=0, tiled=True),
        lax.all_gather(out_bias, "fsdp", axis=0, tiled=True),
        lax.all_gather(out_gain, "fsdp", axis=0, tiled=True),
        lax.all_gather(out_shift, "fsdp", axis=0, tiled=True),
    )
    model_width = layer_input.shape[-1]
    tokens = layer_input.reshape(-1, model_width)
    token_rows = tokens.shape[0]
    tokens_single = tokens.astype(single)
    query_rows = (
        jnp.dot(tokens, full_query, preferred_element_type=single) + bias_query.astype(single)
    ).astype(half)
    key_rows = jnp.dot(tokens, full_key, preferred_element_type=single).astype(half)
    value_rows = (
        jnp.dot(tokens, full_value, preferred_element_type=single) + bias_value.astype(single)
    ).astype(half)
    stacked = jnp.stack([query_rows, key_rows, value_rows])
    regrouped = lax.all_to_all(stacked, "seq", split_axis=2, concat_axis=1, tiled=True)
    seq_length = regrouped.shape[1]
    local_width = regrouped.shape[2]
    heads_here = local_width // HD
    query_heads = regrouped[0].reshape(seq_length, heads_here, HD)
    key_heads = regrouped[1].reshape(seq_length, heads_here, HD)
    value_heads = regrouped[2].reshape(seq_length, heads_here, HD)
    block_rows = min(512, seq_length)
    block_count = seq_length // block_rows
    query_blocks = query_heads.reshape(block_count, block_rows, heads_here, HD)

    def forward_block(query_block):
        scores = (
            jnp.einsum("qhd,khd->hqk", query_block, key_heads, preferred_element_type=single)
            * 0.125
        )
        row_max = jnp.max(scores, axis=-1, keepdims=True)
        exp_scores = jnp.exp(scores - row_max)
        row_total = jnp.sum(exp_scores, axis=-1, keepdims=True)
        attn_probs = exp_scores / row_total
        block_out = jnp.einsum(
            "hqk,khd->qhd", attn_probs.astype(half), value_heads, preferred_element_type=single
        )
        return (block_out.astype(half), row_max[..., 0] + jnp.log(row_total[..., 0]))

    mixed_blocks, log_total = lax.map(forward_block, query_blocks)
    attn_mixed = mixed_blocks.reshape(seq_length, local_width)
    regathered = lax.all_to_all(attn_mixed, "seq", split_axis=0, concat_axis=1, tiled=True)
    attn_out = jnp.dot(regathered, full_output, preferred_element_type=single) + bias_output.astype(
        single
    )
    normed, pull_first = jax.vjp(
        layer_norm, tokens_single + attn_out, gain_one.astype(single), shift_one.astype(single)
    )
    normed_low = normed.astype(half)
    hidden_pre = jnp.dot(normed_low, full_in, preferred_element_type=single) + bias_in.astype(
        single
    )
    hidden_single, pull_gelu = jax.vjp(gelu_exact, hidden_pre)
    hidden = hidden_single.astype(half)
    branch = jnp.dot(hidden, full_out, preferred_element_type=single) + bias_out.astype(single)
    layer_out, pull_second = jax.vjp(
        layer_norm, normed + branch, gain_two.astype(single), shift_two.astype(single)
    )
    squares = jnp.stack(
        [
            jnp.sum(tokens_single * tokens_single),
            jnp.sum(attn_out * attn_out),
            jnp.sum(normed * normed),
            jnp.sum(branch * branch),
            jnp.sum(layer_out * layer_out),
        ]
    )
    square_sums = lax.psum(squares, ("seq", "fsdp"))
    rms_values = jnp.sqrt(square_sums / single(token_rows * model_width * seq_count * fsdp_count))
    cotangent = out_cotangent.reshape(token_rows, model_width).astype(single)
    grad_stream, grad_gain_two, grad_shift_two = pull_second(cotangent)
    grad_branch = grad_stream.astype(half)
    grad_bias_out = column_sums(grad_branch)
    grad_out = jnp.dot(hidden.T, grad_branch, preferred_element_type=single)
    grad_hidden = jnp.dot(grad_branch, full_out.T, preferred_element_type=single)
    grad_pre = pull_gelu(grad_hidden)[0].astype(half)
    grad_bias_in = column_sums(grad_pre)
    grad_in = jnp.dot(normed_low.T, grad_pre, preferred_element_type=single)
    grad_normed = grad_stream + jnp.dot(grad_pre, full_in.T, preferred_element_type=single)
    grad_h, grad_gain_one, grad_shift_one = pull_first(grad_normed)
    mlp_summed = (
        lax.psum_scatter(grad_in, "fsdp", scatter_dimension=0, tiled=True),
        lax.psum_scatter(grad_out, "fsdp", scatter_dimension=0, tiled=True),
        lax.psum_scatter(grad_bias_in, "fsdp", scatter_dimension=0, tiled=True),
        lax.psum_scatter(grad_bias_out, "fsdp", scatter_dimension=0, tiled=True),
        lax.psum_scatter(grad_gain_two, "fsdp", scatter_dimension=0, tiled=True),
        lax.psum_scatter(grad_shift_two, "fsdp", scatter_dimension=0, tiled=True),
    )
    grad_attn = grad_h.astype(half)
    grad_bias_output = column_sums(grad_attn)
    grad_output = jnp.dot(regathered.T, grad_attn, preferred_element_type=single)
    grad_regathered = jnp.dot(grad_attn, full_output.T, preferred_element_type=single).astype(half)
    grad_mixed = lax.all_to_all(grad_regathered, "seq", split_axis=1, concat_axis=0, tiled=True)
    grad_mixed_blocks = grad_mixed.reshape(block_count, block_rows, heads_here, HD)

    def backward_block(grad_carry, block_parts):
        grad_keys, grad_values = grad_carry
        query_block, block_total, grad_block = block_parts
        scores = (
            jnp.einsum("qhd,khd->hqk", query_block, key_heads, preferred_element_type=single)
            * 0.125
        )
        attn_probs = jnp.exp(scores - block_total[..., None])
        grad_probs = jnp.einsum(
            "qhd,khd->hqk", grad_block, value_heads, preferred_element_type=single
        )
        row_delta = jnp.sum(attn_probs * grad_probs, axis=-1, keepdims=True)
        grad_scores = (attn_probs * (grad_probs - row_delta)).astype(half)
        grad_query = (
            jnp.einsum("hqk,khd->qhd", grad_scores, key_heads, preferred_element_type=single)
            * 0.125
        )
        grad_keys = (
            grad_keys
            + jnp.einsum("hqk,qhd->khd", grad_scores, query_block, preferred_element_type=single)
            * 0.125
        )
        grad_values = grad_values + jnp.einsum(
            "hqk,qhd->khd", attn_probs.astype(half), grad_block, preferred_element_type=single
        )
        return ((grad_keys, grad_values), grad_query.astype(half))

    zero_grads = jnp.zeros((seq_length, heads_here, HD), single)
    (grad_keys, grad_values), grad_query_blocks = lax.scan(
        backward_block, (zero_grads, zero_grads), (query_blocks, log_total, grad_mixed_blocks)
    )
    grad_heads = jnp.stack(
        [
            grad_query_blocks.reshape(seq_length, local_width),
            grad_keys.reshape(seq_length, local_width).astype(half),
            grad_values.reshape(seq_length, local_width).astype(half),
        ]
    )
    grad_tokens = lax.all_to_all(grad_heads, "seq", split_axis=1, concat_axis=2, tiled=True)
    grad_query_rows = grad_tokens[0]
    grad_key_rows = grad_tokens[1]
    grad_value_rows = grad_tokens[2]
    grad_query = jnp.dot(tokens.T, grad_query_rows, preferred_element_type=single)
    grad_key = jnp.dot(tokens.T, grad_key_rows, preferred_element_type=single)
    grad_value = jnp.dot(tokens.T, grad_value_rows, preferred_element_type=single)
    grad_bias_query = column_sums(grad_query_rows)
    grad_bias_value = column_sums(grad_value_rows)
    input_grad = grad_h + jnp.dot(grad_query_rows, full_query.T, preferred_element_type=single)
    input_grad = input_grad + jnp.dot(grad_key_rows, full_key.T, preferred_element_type=single)
    input_grad = input_grad + jnp.dot(grad_value_rows, full_value.T, preferred_element_type=single)
    attn_summed = (
        lax.psum_scatter(grad_query, "fsdp", scatter_dimension=0, tiled=True),
        lax.psum_scatter(grad_key, "fsdp", scatter_dimension=0, tiled=True),
        lax.psum_scatter(grad_value, "fsdp", scatter_dimension=0, tiled=True),
        lax.psum_scatter(grad_output, "fsdp", scatter_dimension=0, tiled=True),
        lax.psum_scatter(grad_bias_query, "fsdp", scatter_dimension=0, tiled=True),
        lax.psum_scatter(grad_bias_value, "fsdp", scatter_dimension=0, tiled=True),
        lax.psum_scatter(grad_bias_output, "fsdp", scatter_dimension=0, tiled=True),
        lax.psum_scatter(grad_gain_one, "fsdp", scatter_dimension=0, tiled=True),
        lax.psum_scatter(grad_shift_one, "fsdp", scatter_dimension=0, tiled=True),
    )
    summed = lax.psum(
        (
            attn_summed[0],
            attn_summed[1],
            attn_summed[2],
            attn_summed[3],
            attn_summed[4],
            attn_summed[5],
            attn_summed[6],
            attn_summed[7],
            attn_summed[8],
            mlp_summed[0],
            mlp_summed[1],
            mlp_summed[2],
            mlp_summed[3],
            mlp_summed[4],
            mlp_summed[5],
        ),
        "seq",
    )
    results = (
        summed[0],
        summed[1],
        summed[2],
        summed[3],
        summed[4],
        summed[5],
        summed[6],
        summed[7],
        summed[8],
        summed[9],
        summed[11],
        summed[10],
        summed[12],
        summed[13],
        summed[14],
    )
    return (
        layer_out.astype(half).reshape(layer_input.shape),
        input_grad.reshape(layer_input.shape),
        results[0],
        results[1],
        results[2],
        results[3],
        results[4],
        results[5],
        results[6],
        results[7],
        results[8],
        results[9],
        results[10],
        results[11],
        results[12],
        results[13],
        results[14],
        rms_values,
    )


def solution(mesh):
    placed = (
        P("fsdp", "seq", None),
        P("fsdp", None),
        P("fsdp", None),
        P("fsdp", None),
        P("fsdp", None),
        P("fsdp"),
        P("fsdp"),
        P("fsdp"),
        P("fsdp"),
        P("fsdp"),
        P("fsdp", None),
        P("fsdp"),
        P("fsdp", None),
        P("fsdp"),
        P("fsdp"),
        P("fsdp"),
        P("fsdp", "seq", None),
    )
    return jax.shard_map(
        local,
        mesh=mesh,
        in_specs=placed,
        out_specs=(
            P("fsdp", "seq", None),
            P("fsdp", "seq", None),
            P("fsdp", None),
            P("fsdp", None),
            P("fsdp", None),
            P("fsdp", None),
            P("fsdp"),
            P("fsdp"),
            P("fsdp"),
            P("fsdp"),
            P("fsdp"),
            P("fsdp", None),
            P("fsdp"),
            P("fsdp", None),
            P("fsdp"),
            P("fsdp"),
            P("fsdp"),
            P(),
        ),
        check_vma=False,
    )
```

profile of v0, /device:TPU:0, one launch (start us, length us, event | category | flops | bytes accessed | tf_op | source)
XLA Modules:
  0.0 1655.2 jit_solution(8044954652545755404)
XLA Ops:
  10.6 22.4 %all-gather = bf16[8,1,128]{2,1,0:T(2,128)(2,1)S(1)} all-gather(bf16[1,1,128]{2,1,0:T(2,128)(2,1)} %bitcast.251), channel_id=1, replica_groups=mesh['seq'=4,'fsdp'=8] {'fsdp'}, dimensions={0}, use_global_device_ids=true | all-gather | bytes 2304 | tf_op jit(solution)/shard_map/all_gather | solution.py:61
  32.9 16.5 all-gather.1
  49.5 12.7 all-gather.18.cloned.1.call-done
  65.0 47.1 %all-gather.16.cloned.1.call-done = bf16[1024,1024]{1,0:T(8,128)(2,1)} async-done(((bf16[128,1024]{1,0:T(8,128)(2,1)}), bf16[1024,1024]{1,0:T(8,128)(2,1)}) %all-gather.16.cloned.1.call-update) | async-done | bytes 2097168 | tf_op jit(solution)/shard_map/all_gather | solution.py:57
  115.6 46.5 %all-gather.20.cloned.1.call-done = bf16[1024,1024]{1,0:T(8,128)(2,1)} async-done(((bf16[128,1024]{1,0:T(8,128)(2,1)}), bf16[1024,1024]{1,0:T(8,128)(2,1)}) %all-gather.20.cloned.1.call-update) | async-done | bytes 2097168 | tf_op jit(solution)/shard_map/all_gather | solution.py:59
  173.1 36.3 %all-to-all-done = bf16[3,384,1024]{1,0,2:T(4,128)(2,1)S(1)} async-done(((bf16[3,384,1024]{1,0,2:T(4,128)(2,1)}), bf16[3,384,1024]{1,0,2:T(4,128)(2,1)S(1)}, u32[]{:S(2)}, u32[]{:S(2)}) %all-to-all-start) | async-done | bytes 2359328 | tf_op jit(solution)/shard_map/all_to_all | solution.py:87
  218.6 25.2 %while.27 = (s32[]{:T(128)}, bf16[3,512,4,64]{1,3,2,0:T(8,128)(2,1)}, f32[3,4,512]{2,1,0:T(4,128)S(1)}, bf16[3,512,4,64]{1,3,2,0:T(8,128)(2,1)S(1)}, bf16[1536,4...) while((s32[]{:T(128)}, bf16[3,512,4,64]{1,3,2,0:T(8,128)(2,1)}, ...), condition=%wide.region_3.4_spmd, body=%wide.region_0.3_spmd.sunk | while | flops 833746944 | bytes 39912020 | solution.py:112
  256.5 18.1 %all-gather.2 = bf16[8,1,128]{2,1,0:T(2,128)(2,1)S(1)} all-gather(bf16[1,1,128]{2,1,0:T(2,128)(2,1)S(1)} %bitcast.253), channel_id=1, replica_groups=mesh['seq'=4,'fsdp'=8] {'fsdp'}, dimensions={0}, use_global_device_ids=true | all-gather | bytes 2304 | tf_op jit(solution)/shard_map/all_gather | solution.py:63
  274.6 16.7 %all-gather.3 = bf16[8,1,128]{2,1,0:T(2,128)(2,1)S(1)} all-gather(bf16[1,1,128]{2,1,0:T(2,128)(2,1)S(1)} %bitcast.254), channel_id=1, replica_groups=mesh['seq'=4,'fsdp'=8] {'fsdp'}, dimensions={0}, use_global_device_ids=true | all-gather | bytes 2304 | tf_op jit(solution)/shard_map/all_gather | solution.py:64
  291.3 18.1 %all-gather.4 = bf16[8,1,128]{2,1,0:T(2,128)(2,1)S(1)} all-gather(bf16[1,1,128]{2,1,0:T(2,128)(2,1)S(1)} %bitcast.255), channel_id=1, replica_groups=mesh['seq'=4,'fsdp'=8] {'fsdp'}, dimensions={0}, use_global_device_ids=true | all-gather | bytes 2304 | tf_op jit(solution)/shard_map/all_gather | solution.py:65
  309.4 26.3 %all-gather.5 = bf16[8,1,512]{2,1,0:T(2,128)(2,1)S(1)} all-gather(bf16[1,1,512]{2,1,0:T(2,128)(2,1)S(1)} %reshape.201), channel_id=1, replica_groups=mesh['seq'=4,'fsdp'=8] {'fsdp'}, dimensions={0}, use_global_device_ids=true | all-gather | bytes 9216 | tf_op jit(solution)/shard_map/all_gather | solution.py:70
  335.7 16.3 all-gather.6
  352.0 18.5 %all-gather.7 = bf16[8,1,128]{2,1,0:T(2,128)(2,1)S(1)} all-gather(bf16[1,1,128]{2,1,0:T(2,128)(2,1)S(1)} %bitcast.257), channel_id=1, replica_groups=mesh['seq'=4,'fsdp'=8] {'fsdp'}, dimensions={0}, use_global_device_ids=true | all-gather | bytes 2304 | tf_op jit(solution)/shard_map/all_gather | solution.py:72
  370.5 16.3 all-gather.8
  392.2 21.0 %multiply_convert_fusion.1 = (bf16[384,4096]{1,0:T(8,128)(2,1)}, f32[384,4096]{1,0:T(8,128)}, f32[384,4096]{1,0:T(8,128)}) fusion(f32[4096]{0:T(1024)S(1)} %bitcast.246, bf16[1024,4096]{1,0:T(8,128)(2,1)} %all-gather.24.cloned.1.call-done, f32[384,1024]{1,0:T(8,128)} %copy-done.7, f32[1024]{0:T(1024)S(1)} %bitcast.235, f32[1024]{0:T(1024)S(1)} %bitcast.230, ...), kind=kOutput, calls=%fused_computation.50 | convolution fusion | flops 3327000576 | bytes 25717760 | tf_op jit(solution)/shard_map/dot_general | solution.py:122
  413.2 49.8 %all-gather.26.cloned.1.call-done = bf16[4096,1024]{1,0:T(8,128)(2,1)} async-done(((bf16[512,1024]{1,0:T(8,128)(2,1)}), bf16[4096,1024]{1,0:T(8,128)(2,1)}) %all-gather.26.cloned.1.call-update) | async-done | bytes 8388624 | tf_op jit(solution)/shard_map/all_gather | solution.py:69
  463.0 9.0 fusion.73
  476.0 14.0 convert_reduce_fusion
  511.3 6.9 all-to-all-done.2
  527.8 84.8 %while.28 = (s32[]{:T(128)}, f32[1536,4,64]{0,2,1:T(8,128)}, f32[1536,4,64]{0,2,1:T(8,128)}, bf16[3,512,4,64]{1,3,2,0:T(8,128)(2,1)}, bf16[3,512,4,64]{1,3,2,0:T...) while((s32[]{:T(128)}, f32[1536,4,64]{0,2,1:T(8,128)}, ...), condition=%wide.region_14.15_spmd.clone, body=%wide.region_12.14_spmd.clone.sunk | while | flops 2053240832 | bytes 211347216 | solution.py:196
  623.2 39.6 %all_to_all.65 = bf16[3,1536,256]{2,0,1:T(4,128)(2,1)S(1)} all-to-all(bf16[3,1536,256]{2,0,1:T(4,128)(2,1)S(1)} %copy.76), channel_id=1, replica_groups=mesh['seq'=4,'fsdp'=8] {'seq'}, dimensions={1} | all-to-all | bytes 4718592 | tf_op jit(solution)/shard_map/all_to_all | solution.py:206
  685.0 13.1 fusion.68
  698.4 12.5 fusion.81
  711.0 45.6 %reduce-scatter.11.cloned.1.call-done = f32[128,1024]{0,1:T(8,128)} async-done(((f32[1024,1024]{0,1:T(8,128)}), f32[128,1024]{0,1:T(8,128)}) %reduce-scatter.11.cloned.1.call-update) | async-done | bytes 524304 | tf_op jit(solution)/shard_map/reduce_scatter | solution.py:221
  756.6 91.9 %reduce-scatter.7.cloned.1.call-done = f32[128,1024]{0,1:T(8,128)} async-done(((f32[1024,1024]{0,1:T(8,128)}), f32[128,1024]{0,1:T(8,128)}) %reduce-scatter.7.cloned.1.call-update) | async-done | bytes 524304 | tf_op jit(solution)/shard_map/reduce_scatter | solution.py:219
  848.5 92.2 %reduce-scatter.9.cloned.1.call-done = f32[128,1024]{0,1:T(8,128)} async-done(((f32[1024,1024]{0,1:T(8,128)}), f32[128,1024]{0,1:T(8,128)}) %reduce-scatter.9.cloned.1.call-update) | async-done | bytes 524304 | tf_op jit(solution)/shard_map/reduce_scatter | solution.py:220
  940.7 286.3 %reduce-scatter.15.cloned.1.call-done = f32[128,4096]{1,0:T(8,128)} async-done(((f32[1024,4096]{1,0:T(8,128)}), f32[128,4096]{1,0:T(8,128)}) %reduce-scatter.15.cloned.1.call-update) | async-done | bytes 2097168 | tf_op jit(solution)/shard_map/reduce_scatter | solution.py:154
  1227.0 285.9 %reduce-scatter.17.cloned.1.call-done = f32[512,1024]{1,0:T(8,128)} async-done(((f32[4096,1024]{1,0:T(8,128)}), f32[512,1024]{1,0:T(8,128)}) %reduce-scatter.17.cloned.1.call-update) | async-done | bytes 2097168 | tf_op jit(solution)/shard_map/reduce_scatter | solution.py:155
  1520.0 39.8 %psum.127 = f32[5]{0:T(128)S(1)} all-reduce(f32[5]{0:T(128)S(1)} %stack.45), channel_id=1, replica_groups=mesh['seq'=4,'fsdp'=8] {'seq','fsdp'}, use_global_device_ids=true, to_apply=%region_59.60 | all-reduce | flops 5 | bytes 40 | tf_op jit(solution)/shard_map/psum | solution.py:140
  1560.7 37.3 %all-reduce.9 = (f32[1024]{0:T(1024)S(1)}, f32[1024]{0:T(1024)S(1)}, f32[1024]{0:T(1024)S(1)}, f32[1024]{0:T(1024)S(1)}, f32[1024]{0:T(1024)S(1)}, /*index=5*/f3...) all-reduce(f32[1024]{0:T(1024)S(1)} %bitcast.244, ...), channel_id=6, replica_groups=mesh['seq'=4,'fsdp'=8] {'fsdp'}, use_global_device_ids=true, to_apply=%region_24.25.clone | all-reduce | flops 12288 | bytes 98304
  1598.7 7.0 all-reduce.10
  1613.2 23.7 %all-reduce.14.cloned.1.call-done = (f32[128,1024]{0,1:T(8,128)}, f32[128,1024]{0,1:T(8,128)}, f32[128,1024]{0,1:T(8,128)}, f32[128,1024]{1,0:T(8,128)}, f32[128,4096]{1,0:T(8,128)}, /*index=5*/f32[512,1024]{1,0:T(8,128)}) async-done(((f32[128,1024]{0,1:T(8,128)}, f32[128,1024]{0,1:T(8,128)}, f32[128,1024]{0,1:T(8,128)}, f32[128,1024]{1,0:T(8,128)}, f32[128,4096]{1,0:T(8,128)}, ...) | async-done | bytes 6291472 | tf_op jit(solution)/shard_map/psum | solution.py:229
  (268 shorter events, 251.7 us)
Async XLA Ops:
  7.2 55.0 %all-gather.18.cloned.1.call-start = ((), (), s32[]{:S(2)}) async-start(), calls=%async_computation.11 | async-start | bytes 2359296 | tf_op jit(solution)/shard_map/all_gather | solution.py:58
  7.9 104.2 %all-gather.16.cloned.1.call-start = ((), (), s32[]{:S(2)}) async-start(), calls=%async_computation.10 | async-start | bytes 2359296 | tf_op jit(solution)/shard_map/all_gather | solution.py:57
  8.7 153.4 %all-gather.20.cloned.1.call-start = ((), (), s32[]{:S(2)}) async-start(), calls=%async_computation.12 | async-start | bytes 2359296 | tf_op jit(solution)/shard_map/all_gather | solution.py:59
  9.4 377.5 %all-gather.22.cloned.1.call-start = ((), (), s32[]{:S(2)}) async-start(), calls=%async_computation.13 | async-start | bytes 2359296 | tf_op jit(solution)/shard_map/all_gather | solution.py:60
  10.0 102.1 %copy-start.10 = (bf16[1,384,1024]{2,1,0:T(8,128)(2,1)S(1)}, bf16[1,384,1024]{2,1,0:T(8,128)(2,1)}, u32[]{:S(2)}) copy-start(bf16[1,384,1024]{2,1,0:T(8,128)(2,1)} %param.21) | copy-start | bytes 2359300
  10.0 382.2 %all-gather.24.cloned.1.call-start = ((), (), s32[]{:S(2)}) async-start(), calls=%async_computation.14 | async-start | bytes 9437184 | tf_op jit(solution)/shard_map/all_gather | solution.py:68
  168.8 40.7 %all-to-all-start = ((bf16[3,384,1024]{1,0,2:T(4,128)(2,1)}), bf16[3,384,1024]{1,0,2:T(4,128)(2,1)S(1)}, u32[]{:S(2)}, u32[]{:S(2)}) async-start(bf16[3,384,1024]{1,0,2:T(4,128)(2,1)} %copy.66), calls=%async_computation | async-start | bytes 6291456 | tf_op jit(solution)/shard_map/all_to_all | solution.py:87
  172.5 290.4 %all-gather.26.cloned.1.call-start = ((), (), s32[]{:S(2)}) async-start(), calls=%async_computation.15 | async-start | bytes 9437184 | tf_op jit(solution)/shard_map/all_gather | solution.py:69
  243.8 47.4 %copy-start.38 = (bf16[128]{0:T(256)(128)(2,1)S(1)}, bf16[128]{0:T(256)(128)(2,1)}, u32[]{:S(2)}) copy-start(bf16[128]{0:T(256)(128)(2,1)} %param.30) | copy-start | bytes 772
  243.8 65.5 %copy-start.35 = (bf16[512]{0:T(512)(128)(2,1)S(1)}, bf16[512]{0:T(512)(128)(2,1)}, u32[]{:S(2)}) copy-start(bf16[512]{0:T(512)(128)(2,1)} %param.32) | copy-start | bytes 3076
  243.8 91.9 %copy-start.39 = (bf16[128]{0:T(256)(128)(2,1)S(1)}, bf16[128]{0:T(256)(128)(2,1)}, u32[]{:S(2)}) copy-start(bf16[128]{0:T(256)(128)(2,1)} %param.34) | copy-start | bytes 772
  243.8 108.2 %copy-start.40 = (bf16[128]{0:T(256)(128)(2,1)S(1)}, bf16[128]{0:T(256)(128)(2,1)}, u32[]{:S(2)}) copy-start(bf16[128]{0:T(256)(128)(2,1)} %param.35) | copy-start | bytes 772
  243.9 126.7 %copy-start.41 = (bf16[128]{0:T(256)(128)(2,1)S(1)}, bf16[128]{0:T(256)(128)(2,1)}, u32[]{:S(2)}) copy-start(bf16[128]{0:T(256)(128)(2,1)} %param.36) | copy-start | bytes 772
  252.2 134.6 %all-to-all-start.1 = ((bf16[4,384,256]{1,2,0:T(8,128)(2,1)}), bf16[4,384,256]{1,2,0:T(8,128)(2,1)}, u32[]{:S(2)}, u32[]{:S(2)}) async-start(bf16[4,384,256]{1,2,0:T(8,128)(2,1)} %copy.70), calls=%async_computation.1 | async-start | bytes 1572864 | tf_op jit(solution)/shard_map/all_to_all | solution.py:114
  291.3 203.3 %copy-start.19 = (f32[8,1,128]{2,1,0:T(1,128)}, f32[8,1,128]{2,1,0:T(1,128)S(1)}, u32[]{:S(2)}) copy-start(f32[8,1,128]{2,1,0:T(1,128)S(1)} %convert_element_type.164) | copy-start | bytes 12292
  309.4 180.6 %copy-start.21 = (f32[8,1,128]{2,1,0:T(1,128)}, f32[8,1,128]{2,1,0:T(1,128)S(1)}, u32[]{:S(2)}) copy-start(f32[8,1,128]{2,1,0:T(1,128)S(1)} %convert_element_type.165) | copy-start | bytes 12292
  390.8 103.8 %copy-start.23 = (f32[384]{0:T(512)}, f32[384]{0:T(512)S(1)}, u32[]{:S(2)}) copy-start(f32[384]{0:T(512)S(1)} %broadcast_multiply_fusion.1) | copy-start | bytes 4612
  392.2 102.4 %copy-start.25 = (f32[384]{0:T(512)}, f32[384]{0:T(512)S(1)}, u32[]{:S(2)}) copy-start(f32[384]{0:T(512)S(1)} %fusion.66) | copy-start | bytes 4612
  502.2 15.9 all-to-all-start.2
  506.4 204.5 %reduce-scatter.13.cloned.1.call-start = ((), (), s32[]{:S(2)}) async-start(), calls=%async_computation.19 | async-start | bytes 4718592 | tf_op jit(solution)/shard_map/reduce_scatter | solution.py:222
  511.2 245.4 %reduce-scatter.11.cloned.1.call-start = ((), (), s32[]{:S(2)}) async-start(), calls=%async_computation.18 | async-start | bytes 4718592 | tf_op jit(solution)/shard_map/reduce_scatter | solution.py:221
  670.5 178.0 %reduce-scatter.7.cloned.1.call-start = ((), (), s32[]{:S(2)}) async-start(), calls=%async_computation.16 | async-start | bytes 4718592 | tf_op jit(solution)/shard_map/reduce_scatter | solution.py:219
  677.4 263.2 %reduce-scatter.9.cloned.1.call-start = ((), (), s32[]{:S(2)}) async-start(), calls=%async_computation.17 | async-start | bytes 4718592 | tf_op jit(solution)/shard_map/reduce_scatter | solution.py:220
  684.4 542.6 %reduce-scatter.15.cloned.1.call-start = ((), (), s32[]{:S(2)}) async-start(), calls=%async_computation.20 | async-start | bytes 18874368 | tf_op jit(solution)/shard_map/reduce_scatter | solution.py:154
  698.1 814.8 %reduce-scatter.17.cloned.1.call-start = ((), (), s32[]{:S(2)}) async-start(), calls=%async_computation.21 | async-start | bytes 18874368 | tf_op jit(solution)/shard_map/reduce_scatter | solution.py:155
  710.9 926.0 %all-reduce.14.cloned.1.call-start = ((), (), s32[]{:S(2)}) async-start(), calls=%async_computation.22 | async-start | bytes 12582912 | tf_op jit(solution)/shard_map/psum | solution.py:229
  1512.9 47.7 %copy-start.29 = (f32[1024]{0:T(1024)S(1)}, f32[1024]{0:T(1024)}, u32[]{:S(2)}) copy-start(f32[1024]{0:T(1024)} %get-tuple-element.254) | copy-start | bytes 12292
  1512.9 47.8 %copy-start.30 = (f32[1024]{0:T(1024)S(1)}, f32[1024]{0:T(1024)}, u32[]{:S(2)}) copy-start(f32[1024]{0:T(1024)} %get-tuple-element.315) | copy-start | bytes 12292
  1512.9 47.8 %copy-start.31 = (f32[1024]{0:T(1024)S(1)}, f32[1024]{0:T(1024)}, u32[]{:S(2)}) copy-start(f32[1024]{0:T(1024)} %get-tuple-element.319) | copy-start | bytes 12292
  1512.9 47.8 %copy-start.32 = (f32[4096]{0:T(1024)S(1)}, f32[4096]{0:T(1024)}, u32[]{:S(2)}) copy-start(f32[4096]{0:T(1024)} %get-tuple-element.317) | copy-start | bytes 49156
  1512.9 47.8 %copy-start.33 = (f32[1024]{0:T(1024)S(1)}, f32[1024]{0:T(1024)}, u32[]{:S(2)}) copy-start(f32[1024]{0:T(1024)} %get-tuple-element.252) | copy-start | bytes 12292
  1512.9 47.8 %copy-start.34 = (f32[1024]{0:T(1024)S(1)}, f32[1024]{0:T(1024)}, u32[]{:S(2)}) copy-start(f32[1024]{0:T(1024)} %get-tuple-element.260) | copy-start | bytes 12292
  (39 other events, 230.0 us)
Sparse Core Ops, SparseCore 0:
  10.1 51.9 all-gather.17
  64.3 47.7 all-gather.15
  114.3 47.7 all-gather.19
  164.0 47.7 all-gather.21
  213.8 123.6 all-gather.23
  339.5 123.4 all-gather.25
  511.3 86.5 reduce-scatter.12
  670.6 85.9 reduce-scatter.10
  760.2 88.2 reduce-scatter.6
  852.4 88.2 reduce-scatter.8
  944.4 282.4 reduce-scatter.14
  1231.1 281.7 reduce-scatter.16
  1515.7 121.1 all-reduce.13
where the time goes:
time: 1660 us
  waiting for transfers between devices  1030 us (62%)
  blocking collectives  293 us (18%)
  matrix products  203 us (12%)
  local copies, waits for them, and re-layouts  70.2 us (4%)
  other arithmetic  31.7 us (2%)
    reduce_scatter x1, waiting for transfers between devices, local(): lax.psum_scatter(grad_in, 'fsdp', scatter_dimension=0, tiled=True)  286 us
    reduce_scatter x1, waiting for transfers between devices, local(): lax.psum_scatter(grad_out, 'fsdp', scatter_dimension=0, tiled=True)  286 us
    reduce_scatter x1, waiting for transfers between devices, local(): lax.psum_scatter(grad_key, 'fsdp', scatter_dimension=0, tiled=True)  92.2 us
    reduce_scatter x1, waiting for transfers between devices, local(): lax.psum_scatter(grad_query, 'fsdp', scatter_dimension=0, tiled=True)  91.9 us
    all_gather x1, waiting for transfers between devices, local(): lax.all_gather(out_weight, 'fsdp', axis=0, tiled=True)  49.8 us
    all_gather x1, waiting for transfers between devices, local(): lax.all_gather(query_weight, 'fsdp', axis=0, tiled=True)  47.1 us
    all_gather x1, waiting for transfers between devices, local(): lax.all_gather(value_weight, 'fsdp', axis=0, tiled=True)  46.5 us
    reduce_scatter x1, waiting for transfers between devices, local(): lax.psum_scatter(grad_value, 'fsdp', scatter_dimension=0, tiled=True)  45.6 us
  transfers between devices with their start and end apart: 16, of which 12 were waited for; matrix products, arithmetic and copies ran while one was open for 15% of the time, Pallas kernels for 0%

commit v1 on v0

--- a/solution.py
+++ b/solution.py
@@ -137,7 +137,7 @@
             jnp.sum(layer_out * layer_out),
         ]
     )
-    square_sums = lax.psum(squares, ("seq", "fsdp"))
+    square_sums = lax.psum(lax.psum(squares, "fsdp"), "seq")
     rms_values = jnp.sqrt(square_sums / single(token_rows * model_width * seq_count * fsdp_count))
     cotangent = out_cotangent.reshape(token_rows, model_width).astype(single)
     grad_stream, grad_gain_two, grad_shift_two = pull_second(cotangent)

time: 1660 us -> 1660 us (level)
  blocking collectives: 293 us -> 252 us
  waiting for transfers between devices: 1030 us -> 1070 us
    psum x1 -> x0, blocking collectives: 39.8 us -> none  [local(): square_sums = lax.psum(squares, ('seq', 'fsdp'))]
    psum x1, waiting for transfers between devices: 23.7 us -> 63.3 us  [local(): lax.psum((attn_summed[0], attn_summed[1], attn_summed[2], attn_summed[3],...]
where the time goes in v1:
time: 1660 us; the launch traced here: 1650 us
  waiting for transfers between devices  1070 us (64%)
  blocking collectives  252 us (15%)
  matrix products  203 us (12%)
  local copies, waits for them, and re-layouts  70.3 us (4%)
  other arithmetic  31.8 us (2%)
    reduce_scatter x1, waiting for transfers between devices, local(): lax.psum_scatter(grad_in, 'fsdp', scatter_dimension=0, tiled=True)  286 us
    reduce_scatter x1, waiting for transfers between devices, local(): lax.psum_scatter(grad_out, 'fsdp', scatter_dimension=0, tiled=True)  286 us
    reduce_scatter x1, waiting for transfers between devices, local(): lax.psum_scatter(grad_key, 'fsdp', scatter_dimension=0, tiled=True)  92.2 us
    reduce_scatter x1, waiting for transfers between devices, local(): lax.psum_scatter(grad_query, 'fsdp', scatter_dimension=0, tiled=True)  91.9 us
    psum x1, waiting for transfers between devices, local(): lax.psum((attn_summed[0], attn_summed[1], attn_summed[2], attn_summed[3],...  63.3 us
    all_gather x1, waiting for transfers between devices, local(): lax.all_gather(out_weight, 'fsdp', axis=0, tiled=True)  49.8 us
    all_gather x1, waiting for transfers between devices, local(): lax.all_gather(query_weight, 'fsdp', axis=0, tiled=True)  47.1 us
    all_gather x1, waiting for transfers between devices, local(): lax.all_gather(value_weight, 'fsdp', axis=0, tiled=True)  46.5 us
  transfers between devices with their start and end apart: 16, of which 12 were waited for; matrix products, arithmetic and copies ran while one was open for 15% of the time, Pallas kernels for 0%

profile of v1, /device:TPU:0, one launch (start us, length us, event | category | flops | bytes accessed | tf_op | source)
XLA Modules:
  0.0 1653.7 jit_solution(118266698120691608)
XLA Ops:
  10.6 22.4 %all-gather = bf16[8,1,128]{2,1,0:T(2,128)(2,1)S(1)} all-gather(bf16[1,1,128]{2,1,0:T(2,128)(2,1)} %bitcast.251), channel_id=1, replica_groups=mesh['seq'=4,'fsdp'=8] {'fsdp'}, dimensions={0}, use_global_device_ids=true | all-gather | bytes 2304 | tf_op jit(solution)/shard_map/all_gather | solution.py:61
  32.9 16.5 all-gather.1
  49.5 12.7 all-gather.18.cloned.1.call-done
  65.0 47.1 %all-gather.16.cloned.1.call-done = bf16[1024,1024]{1,0:T(8,128)(2,1)} async-done(((bf16[128,1024]{1,0:T(8,128)(2,1)}), bf16[1024,1024]{1,0:T(8,128)(2,1)}) %all-gather.16.cloned.1.call-update) | async-done | bytes 2097168 | tf_op jit(solution)/shard_map/all_gather | solution.py:57
  115.6 46.5 %all-gather.20.cloned.1.call-done = bf16[1024,1024]{1,0:T(8,128)(2,1)} async-done(((bf16[128,1024]{1,0:T(8,128)(2,1)}), bf16[1024,1024]{1,0:T(8,128)(2,1)}) %all-gather.20.cloned.1.call-update) | async-done | bytes 2097168 | tf_op jit(solution)/shard_map/all_gather | solution.py:59
  173.1 36.3 %all-to-all-done = bf16[3,384,1024]{1,0,2:T(4,128)(2,1)S(1)} async-done(((bf16[3,384,1024]{1,0,2:T(4,128)(2,1)}), bf16[3,384,1024]{1,0,2:T(4,128)(2,1)S(1)}, u32[]{:S(2)}, u32[]{:S(2)}) %all-to-all-start) | async-done | bytes 2359328 | tf_op jit(solution)/shard_map/all_to_all | solution.py:87
  218.6 25.2 %while.27 = (s32[]{:T(128)}, bf16[3,512,4,64]{1,3,2,0:T(8,128)(2,1)}, f32[3,4,512]{2,1,0:T(4,128)S(1)}, bf16[3,512,4,64]{1,3,2,0:T(8,128)(2,1)S(1)}, bf16[1536,4...) while((s32[]{:T(128)}, bf16[3,512,4,64]{1,3,2,0:T(8,128)(2,1)}, ...), condition=%wide.region_3.4_spmd, body=%wide.region_0.3_spmd.sunk | while | flops 833746944 | bytes 39912020 | solution.py:112
  256.5 18.1 %all-gather.2 = bf16[8,1,128]{2,1,0:T(2,128)(2,1)S(1)} all-gather(bf16[1,1,128]{2,1,0:T(2,128)(2,1)S(1)} %bitcast.253), channel_id=1, replica_groups=mesh['seq'=4,'fsdp'=8] {'fsdp'}, dimensions={0}, use_global_device_ids=true | all-gather | bytes 2304 | tf_op jit(solution)/shard_map/all_gather | solution.py:63
  274.5 16.7 %all-gather.3 = bf16[8,1,128]{2,1,0:T(2,128)(2,1)S(1)} all-gather(bf16[1,1,128]{2,1,0:T(2,128)(2,1)S(1)} %bitcast.254), channel_id=1, replica_groups=mesh['seq'=4,'fsdp'=8] {'fsdp'}, dimensions={0}, use_global_device_ids=true | all-gather | bytes 2304 | tf_op jit(solution)/shard_map/all_gather | solution.py:64
  291.3 18.1 %all-gather.4 = bf16[8,1,128]{2,1,0:T(2,128)(2,1)S(1)} all-gather(bf16[1,1,128]{2,1,0:T(2,128)(2,1)S(1)} %bitcast.255), channel_id=1, replica_groups=mesh['seq'=4,'fsdp'=8] {'fsdp'}, dimensions={0}, use_global_device_ids=true | all-gather | bytes 2304 | tf_op jit(solution)/shard_map/all_gather | solution.py:65
  309.4 26.3 %all-gather.5 = bf16[8,1,512]{2,1,0:T(2,128)(2,1)S(1)} all-gather(bf16[1,1,512]{2,1,0:T(2,128)(2,1)S(1)} %reshape.201), channel_id=1, replica_groups=mesh['seq'=4,'fsdp'=8] {'fsdp'}, dimensions={0}, use_global_device_ids=true | all-gather | bytes 9216 | tf_op jit(solution)/shard_map/all_gather | solution.py:70
  335.7 16.3 all-gather.6
  352.0 18.5 %all-gather.7 = bf16[8,1,128]{2,1,0:T(2,128)(2,1)S(1)} all-gather(bf16[1,1,128]{2,1,0:T(2,128)(2,1)S(1)} %bitcast.257), channel_id=1, replica_groups=mesh['seq'=4,'fsdp'=8] {'fsdp'}, dimensions={0}, use_global_device_ids=true | all-gather | bytes 2304 | tf_op jit(solution)/shard_map/all_gather | solution.py:72
  370.5 16.3 all-gather.8
  392.2 20.9 %multiply_convert_fusion.1 = (bf16[384,4096]{1,0:T(8,128)(2,1)}, f32[384,4096]{1,0:T(8,128)}, f32[384,4096]{1,0:T(8,128)}) fusion(f32[4096]{0:T(1024)S(1)} %bitcast.246, bf16[1024,4096]{1,0:T(8,128)(2,1)} %all-gather.24.cloned.1.call-done, f32[384,1024]{1,0:T(8,128)} %copy-done.7, f32[1024]{0:T(1024)S(1)} %bitcast.235, f32[1024]{0:T(1024)S(1)} %bitcast.230, ...), kind=kOutput, calls=%fused_computation.50 | convolution fusion | flops 3327000576 | bytes 25717760 | tf_op jit(solution)/shard_map/dot_general | solution.py:122
  413.2 49.8 %all-gather.26.cloned.1.call-done = bf16[4096,1024]{1,0:T(8,128)(2,1)} async-done(((bf16[512,1024]{1,0:T(8,128)(2,1)}), bf16[4096,1024]{1,0:T(8,128)(2,1)}) %all-gather.26.cloned.1.call-update) | async-done | bytes 8388624 | tf_op jit(solution)/shard_map/all_gather | solution.py:69
  463.0 9.0 fusion.73
  476.0 14.0 convert_reduce_fusion
  511.2 6.9 all-to-all-done.2
  527.9 84.8 %while.28 = (s32[]{:T(128)}, f32[1536,4,64]{0,2,1:T(8,128)}, f32[1536,4,64]{0,2,1:T(8,128)}, bf16[3,512,4,64]{1,3,2,0:T(8,128)(2,1)}, bf16[3,512,4,64]{1,3,2,0:T...) while((s32[]{:T(128)}, f32[1536,4,64]{0,2,1:T(8,128)}, ...), condition=%wide.region_14.15_spmd.clone, body=%wide.region_12.14_spmd.clone.sunk | while | flops 2053240832 | bytes 211347216 | solution.py:196
  544.6 6.4 fusion.150
  623.3 39.6 %all_to_all.65 = bf16[3,1536,256]{2,0,1:T(4,128)(2,1)S(1)} all-to-all(bf16[3,1536,256]{2,0,1:T(4,128)(2,1)S(1)} %copy.76), channel_id=1, replica_groups=mesh['seq'=4,'fsdp'=8] {'seq'}, dimensions={1} | all-to-all | bytes 4718592 | tf_op jit(solution)/shard_map/all_to_all | solution.py:206
  685.1 13.1 fusion.68
  698.5 12.5 fusion.81
  711.0 45.6 %reduce-scatter.11.cloned.1.call-done = f32[128,1024]{0,1:T(8,128)} async-done(((f32[1024,1024]{0,1:T(8,128)}), f32[128,1024]{0,1:T(8,128)}) %reduce-scatter.11.cloned.1.call-update) | async-done | bytes 524304 | tf_op jit(solution)/shard_map/reduce_scatter | solution.py:221
  756.6 91.9 %reduce-scatter.7.cloned.1.call-done = f32[128,1024]{0,1:T(8,128)} async-done(((f32[1024,1024]{0,1:T(8,128)}), f32[128,1024]{0,1:T(8,128)}) %reduce-scatter.7.cloned.1.call-update) | async-done | bytes 524304 | tf_op jit(solution)/shard_map/reduce_scatter | solution.py:219
  848.5 92.2 %reduce-scatter.9.cloned.1.call-done = f32[128,1024]{0,1:T(8,128)} async-done(((f32[1024,1024]{0,1:T(8,128)}), f32[128,1024]{0,1:T(8,128)}) %reduce-scatter.9.cloned.1.call-update) | async-done | bytes 524304 | tf_op jit(solution)/shard_map/reduce_scatter | solution.py:220
  940.7 286.2 %reduce-scatter.15.cloned.1.call-done = f32[128,4096]{1,0:T(8,128)} async-done(((f32[1024,4096]{1,0:T(8,128)}), f32[128,4096]{1,0:T(8,128)}) %reduce-scatter.15.cloned.1.call-update) | async-done | bytes 2097168 | tf_op jit(solution)/shard_map/reduce_scatter | solution.py:154
  1226.9 285.9 %reduce-scatter.17.cloned.1.call-done = f32[512,1024]{1,0:T(8,128)} async-done(((f32[4096,1024]{1,0:T(8,128)}), f32[512,1024]{1,0:T(8,128)}) %reduce-scatter.17.cloned.1.call-update) | async-done | bytes 2097168 | tf_op jit(solution)/shard_map/reduce_scatter | solution.py:155
  1520.2 35.7 %all-reduce.9 = (f32[1024]{0:T(1024)S(1)}, f32[1024]{0:T(1024)S(1)}, f32[1024]{0:T(1024)S(1)}, f32[1024]{0:T(1024)S(1)}, f32[1024]{0:T(1024)S(1)}, /*index=5*/f3...) all-reduce(f32[1024]{0:T(1024)S(1)} %bitcast.244, ...), channel_id=6, replica_groups=mesh['seq'=4,'fsdp'=8] {'fsdp'}, use_global_device_ids=true, to_apply=%region_24.25.clone | all-reduce | flops 12293 | bytes 98344
  1556.6 7.4 all-reduce.10
  1572.1 63.3 %all-reduce.14.cloned.1.call-done = (f32[128,1024]{0,1:T(8,128)}, f32[128,1024]{0,1:T(8,128)}, f32[128,1024]{0,1:T(8,128)}, f32[128,1024]{1,0:T(8,128)}, f32[128,4096]{1,0:T(8,128)}, /*index=5*/f32[512,1024]{1,0:T(8,128)}) async-done(((f32[128,1024]{0,1:T(8,128)}, f32[128,1024]{0,1:T(8,128)}, f32[128,1024]{0,1:T(8,128)}, f32[128,1024]{1,0:T(8,128)}, f32[128,4096]{1,0:T(8,128)}, ...) | async-done | bytes 6291472 | tf_op jit(solution)/shard_map/psum | solution.py:229
  (267 shorter events, 245.4 us)
Async XLA Ops:
  7.2 55.0 %all-gather.18.cloned.1.call-start = ((), (), s32[]{:S(2)}) async-start(), calls=%async_computation.11 | async-start | bytes 2359296 | tf_op jit(solution)/shard_map/all_gather | solution.py:58
  7.9 104.2 %all-gather.16.cloned.1.call-start = ((), (), s32[]{:S(2)}) async-start(), calls=%async_computation.10 | async-start | bytes 2359296 | tf_op jit(solution)/shard_map/all_gather | solution.py:57
  8.7 153.4 %all-gather.20.cloned.1.call-start = ((), (), s32[]{:S(2)}) async-start(), calls=%async_computation.12 | async-start | bytes 2359296 | tf_op jit(solution)/shard_map/all_gather | solution.py:59
  9.4 377.5 %all-gather.22.cloned.1.call-start = ((), (), s32[]{:S(2)}) async-start(), calls=%async_computation.13 | async-start | bytes 2359296 | tf_op jit(solution)/shard_map/all_gather | solution.py:60
  10.0 102.1 %copy-start.10 = (bf16[1,384,1024]{2,1,0:T(8,128)(2,1)S(1)}, bf16[1,384,1024]{2,1,0:T(8,128)(2,1)}, u32[]{:S(2)}) copy-start(bf16[1,384,1024]{2,1,0:T(8,128)(2,1)} %param.21) | copy-start | bytes 2359300
  10.0 382.2 %all-gather.24.cloned.1.call-start = ((), (), s32[]{:S(2)}) async-start(), calls=%async_computation.14 | async-start | bytes 9437184 | tf_op jit(solution)/shard_map/all_gather | solution.py:68
  168.8 40.7 %all-to-all-start = ((bf16[3,384,1024]{1,0,2:T(4,128)(2,1)}), bf16[3,384,1024]{1,0,2:T(4,128)(2,1)S(1)}, u32[]{:S(2)}, u32[]{:S(2)}) async-start(bf16[3,384,1024]{1,0,2:T(4,128)(2,1)} %copy.66), calls=%async_computation | async-start | bytes 6291456 | tf_op jit(solution)/shard_map/all_to_all | solution.py:87
  172.5 290.4 %all-gather.26.cloned.1.call-start = ((), (), s32[]{:S(2)}) async-start(), calls=%async_computation.15 | async-start | bytes 9437184 | tf_op jit(solution)/shard_map/all_gather | solution.py:69
  243.8 12.6 copy-start.36
  243.8 30.7 %copy-start.37 = (bf16[128]{0:T(256)(128)(2,1)S(1)}, bf16[128]{0:T(256)(128)(2,1)}, u32[]{:S(2)}) copy-start(bf16[128]{0:T(256)(128)(2,1)} %param.29) | copy-start | bytes 772
  243.8 47.4 %copy-start.38 = (bf16[128]{0:T(256)(128)(2,1)S(1)}, bf16[128]{0:T(256)(128)(2,1)}, u32[]{:S(2)}) copy-start(bf16[128]{0:T(256)(128)(2,1)} %param.30) | copy-start | bytes 772
  243.8 65.5 %copy-start.35 = (bf16[512]{0:T(512)(128)(2,1)S(1)}, bf16[512]{0:T(512)(128)(2,1)}, u32[]{:S(2)}) copy-start(bf16[512]{0:T(512)(128)(2,1)} %param.32) | copy-start | bytes 3076
  243.8 91.9 %copy-start.39 = (bf16[128]{0:T(256)(128)(2,1)S(1)}, bf16[128]{0:T(256)(128)(2,1)}, u32[]{:S(2)}) copy-start(bf16[128]{0:T(256)(128)(2,1)} %param.34) | copy-start | bytes 772
  243.8 108.1 %copy-start.40 = (bf16[128]{0:T(256)(128)(2,1)S(1)}, bf16[128]{0:T(256)(128)(2,1)}, u32[]{:S(2)}) copy-start(bf16[128]{0:T(256)(128)(2,1)} %param.35) | copy-start | bytes 772
  243.9 126.7 %copy-start.41 = (bf16[128]{0:T(256)(128)(2,1)S(1)}, bf16[128]{0:T(256)(128)(2,1)}, u32[]{:S(2)}) copy-start(bf16[128]{0:T(256)(128)(2,1)} %param.36) | copy-start | bytes 772
  252.2 134.6 %all-to-all-start.1 = ((bf16[4,384,256]{1,2,0:T(8,128)(2,1)}), bf16[4,384,256]{1,2,0:T(8,128)(2,1)}, u32[]{:S(2)}, u32[]{:S(2)}) async-start(bf16[4,384,256]{1,2,0:T(8,128)(2,1)} %copy.70), calls=%async_computation.1 | async-start | bytes 1572864 | tf_op jit(solution)/shard_map/all_to_all | solution.py:114
  291.3 203.3 %copy-start.19 = (f32[8,1,128]{2,1,0:T(1,128)}, f32[8,1,128]{2,1,0:T(1,128)S(1)}, u32[]{:S(2)}) copy-start(f32[8,1,128]{2,1,0:T(1,128)S(1)} %convert_element_type.164) | copy-start | bytes 12292
  309.4 180.6 %copy-start.21 = (f32[8,1,128]{2,1,0:T(1,128)}, f32[8,1,128]{2,1,0:T(1,128)S(1)}, u32[]{:S(2)}) copy-start(f32[8,1,128]{2,1,0:T(1,128)S(1)} %convert_element_type.165) | copy-start | bytes 12292
  390.8 103.8 %copy-start.23 = (f32[384]{0:T(512)}, f32[384]{0:T(512)S(1)}, u32[]{:S(2)}) copy-start(f32[384]{0:T(512)S(1)} %broadcast_multiply_fusion.1) | copy-start | bytes 4612
  392.2 102.4 %copy-start.25 = (f32[384]{0:T(512)}, f32[384]{0:T(512)S(1)}, u32[]{:S(2)}) copy-start(f32[384]{0:T(512)S(1)} %fusion.66) | copy-start | bytes 4612
  474.6 15.4 slice-start
  476.0 14.0 copy-start.12
  476.0 14.0 copy-start.8
  476.0 14.0 slice-start.1
  502.2 15.9 all-to-all-start.2
  506.4 204.6 %reduce-scatter.13.cloned.1.call-start = ((), (), s32[]{:S(2)}) async-start(), calls=%async_computation.19 | async-start | bytes 4718592 | tf_op jit(solution)/shard_map/reduce_scatter | solution.py:222
  511.2 245.4 %reduce-scatter.11.cloned.1.call-start = ((), (), s32[]{:S(2)}) async-start(), calls=%async_computation.18 | async-start | bytes 4718592 | tf_op jit(solution)/shard_map/reduce_scatter | solution.py:221
  670.5 178.0 %reduce-scatter.7.cloned.1.call-start = ((), (), s32[]{:S(2)}) async-start(), calls=%async_computation.16 | async-start | bytes 4718592 | tf_op jit(solution)/shard_map/reduce_scatter | solution.py:219
  677.5 263.2 %reduce-scatter.9.cloned.1.call-start = ((), (), s32[]{:S(2)}) async-start(), calls=%async_computation.17 | async-start | bytes 4718592 | tf_op jit(solution)/shard_map/reduce_scatter | solution.py:220
  684.4 542.4 %reduce-scatter.15.cloned.1.call-start = ((), (), s32[]{:S(2)}) async-start(), calls=%async_computation.20 | async-start | bytes 18874368 | tf_op jit(solution)/shard_map/reduce_scatter | solution.py:154
  698.2 814.6 %reduce-scatter.17.cloned.1.call-start = ((), (), s32[]{:S(2)}) async-start(), calls=%async_computation.21 | async-start | bytes 18874368 | tf_op jit(solution)/shard_map/reduce_scatter | solution.py:155
  710.9 924.5 %all-reduce.14.cloned.1.call-start = ((), (), s32[]{:S(2)}) async-start(), calls=%async_computation.22 | async-start | bytes 12582912 | tf_op jit(solution)/shard_map/psum | solution.py:229
  (39 other events, 173.6 us)
Sparse Core Ops, SparseCore 0:
  10.1 51.9 all-gather.17
  64.3 47.7 all-gather.15
  114.3 47.7 all-gather.19
  164.0 47.7 all-gather.21
  213.8 123.6 all-gather.23
  339.5 123.4 all-gather.25
  511.3 86.6 reduce-scatter.12
  670.7 85.9 reduce-scatter.10
  760.3 88.2 reduce-scatter.6
  852.4 88.1 reduce-scatter.8
  944.5 282.3 reduce-scatter.14
  1231.0 281.7 reduce-scatter.16
  1515.5 119.8 all-reduce.13
